TPU v7x, 256 devices: a whole 4x4x8 slice. The times are simulated.
256 devices in a mesh: rep: 8 (over y, x_hi), blk: 32 (over z, x_lo, core).
Axes of the slice: x: 4 (x_hi: 2, x_lo: 2; x = x_hi * 2 + x_lo), y: 4, z: 8, core: 2. Of those that a mesh axis runs over, the one named last changes fastest.
Arguments:
- node_features: bfloat16 [65536, 256], P(('rep', 'blk')), may hold values from -6 to 6
- tile_values: bfloat16 [8, 32, 128, 128, 128], P('rep', 'blk'), may hold values from -0.09375 to 0.09375
- tile_row: int32 [8, 32, 128], P('rep', 'blk'), may hold values from 0 to 15, as said below
- tile_col: int32 [8, 32, 128], P('rep', 'blk'), may hold values from 0 to 63
- tile_count: int32 [8, 32], P('rep', 'blk'), may hold values from 16 to 128, as said below
- weight: bfloat16 [256, 256], replicated, may hold values from -0.375 to 0.375
- cotangent: bfloat16 [32, 8, 256, 256], P('blk', 'rep'), may hold values from -6 to 6
Outputs:
- layer_out: bfloat16 [32, 8, 256, 256], P('blk', 'rep')
- grad_weight: float32 [256, 256], replicated
- grad_features: bfloat16 [65536, 256], P(('rep', 'blk'))
Inputs may be any that keep to these rules, and one draw needn't show every extreme that they name: `tile_row`: within one device the live slots name distinct tile pairs. Slots 0 to tile_count - 1 of a device are live, the rest are ignored; some device has all 128 slots live.
All inputs are finite; a program needn't handle non-finite values.
Results may differ from a plain program's by a relative error of at most 0.03.
Values may be sent and summed in bfloat16 or wider, within the bound.
No kernel may reach another device: no remote copies, remote signals or barrier semaphores. Data moves between devices by JAX's collectives and lax.ppermute only.
A program may use at most 128 MiB of HBM per device.

v0:
```python
import jax
import jax.numpy as jnp
from jax import lax
from jax.sharding import PartitionSpec as P


def on_device(node_features, tile_values, tile_row, tile_col, tile_count, weight, cotangent):
    rows_dev, features = node_features.shape
    tile_block = tile_values[0, 0]
    slot_rows = tile_row[0, 0]
    slot_cols = tile_col[0, 0]
    live_count = tile_count[0, 0]
    slot_count = tile_block.shape[0]
    tile_size = tile_block.shape[1]
    rep_size = lax.axis_size("rep")
    slab_rows = rows_dev * rep_size
    slab_blocks = slab_rows // tile_size
    live_mask = (jnp.arange(slot_count, dtype=jnp.int32) < live_count).astype(jnp.float32)
    row_hot = (slot_rows[:, None] == jnp.arange(slab_blocks, dtype=jnp.int32)[None, :]).astype(
        jnp.float32
    ) * live_mask[:, None]
    gathered = lax.all_gather(node_features, "blk", axis=0, tiled=True)
    group_blocks = gathered.shape[0] // tile_size
    col_hot = (slot_cols[:, None] == jnp.arange(group_blocks, dtype=jnp.int32)[None, :]).astype(
        jnp.float32
    ) * live_mask[:, None]
    col_blocks = gathered.reshape(group_blocks, tile_size, features)
    picked = jnp.take(col_blocks, slot_cols, axis=0)
    products = jnp.einsum("tij,tjf->tif", tile_block, picked, preferred_element_type=jnp.float32)
    partial_value = (
        jnp.einsum("tk,tif->kif", row_hot, products)
        .reshape(slab_rows, features)
        .astype(jnp.bfloat16)
    )
    hidden_rows = (
        lax.psum_scatter(partial_value, "rep", scatter_dimension=0, tiled=True)
        .astype(jnp.float32)
        .astype(jnp.bfloat16)
    )
    preact = jnp.dot(hidden_rows, weight, preferred_element_type=jnp.float32)
    gating = jax.nn.sigmoid(preact)
    layer_out = (preact * gating).astype(jnp.bfloat16)
    slope_term = gating * (1.0 + preact * (1.0 - gating))
    grad_pre = (cotangent[0, 0].astype(jnp.float32) * slope_term).astype(jnp.bfloat16)
    weight_part = jnp.einsum("nf,ng->fg", hidden_rows, grad_pre, preferred_element_type=jnp.float32)
    grad_hidden = jnp.dot(grad_pre, weight.T, preferred_element_type=jnp.float32).astype(
        jnp.bfloat16
    )
    grad_slab = lax.all_gather(grad_hidden, "rep", axis=0, tiled=True)
    grad_weight = lax.psum(weight_part, ("rep", "blk"))
    grad_blocks = grad_slab.reshape(slab_blocks, tile_size, features)
    picked_rows = jnp.take(grad_blocks, slot_rows, axis=0)
    back_terms = jnp.einsum(
        "tij,tif->tjf", tile_block, picked_rows, preferred_element_type=jnp.float32
    )
    column_terms = (
        jnp.einsum("tk,tjf->kjf", col_hot, back_terms)
        .reshape(group_blocks * tile_size, features)
        .astype(jnp.bfloat16)
    )
    grad_features = (
        lax.psum_scatter(column_terms, "blk", scatter_dimension=0, tiled=True)
        .astype(jnp.float32)
        .astype(jnp.bfloat16)
    )
    return (layer_out.reshape(1, 1, rows_dev, features), grad_weight, grad_features)


def solution(mesh):
    placed = (
        P(("rep", "blk"), None),
        P("rep", "blk", None, None, None),
        P("rep", "blk", None),
        P("rep", "blk", None),
        P("rep", "blk"),
        P(),
        P("blk", "rep", None, None),
    )
    return jax.shard_map(
        on_device,
        mesh=mesh,
        in_specs=placed,
        out_specs=(P("blk", "rep", None, None), P(), P(("rep", "blk"), None)),
        check_vma=False,
    )
```

profile of v0, /device:TPU:24, one launch (start us, length us, event | category | flops | bytes accessed | tf_op | source)
XLA Modules:
  0.0 638.3 jit_solution(16897174415970150977)
XLA Ops:
  7.2 0.0 copy-start
  7.2 0.0 all-gather.3.cloned.1.call-start
  7.2 0.7 all-gather.3.cloned.1.call-update
  7.9 0.0 reduce-scatter.3.cloned.1.call-start
  8.6 0.7 fusion.32
  9.3 0.7 compare_and_fusion.1
  9.9 69.5 %all-gather.3.cloned.1.call-done = bf16[8192,256]{1,0:T(8,128)(2,1)} async-done(((bf16[256,256]{1,0:T(8,128)(2,1)}), bf16[8192,256]{1,0:T(8,128)(2,1)}) %all-gather.3.cloned.1.call-update) | async-done | bytes 4194320 | tf_op jit(solution)/shard_map/all_gather | solution.py:22
  79.4 8.8 %gather_fusion = bf16[128,128,256]{2,1,0:T(8,128)(2,1)} fusion(bf16[64,128,256]{2,1,0:T(8,128)(2,1)} %bitcast.51, s32[1024]{0:T(1024)S(1)} %pad_clamp_fusion.1), kind=kCustom, calls=%fused_computation | custom fusion | bytes 16777728 | tf_op jit(solution)/shard_map/jit(_take)/gather | solution.py:28
  88.2 11.9 %fusion.6 = bf16[128,256,128]{2,1,0:T(8,128)(2,1)} fusion(bf16[128,128,256]{2,1,0:T(8,128)(2,1)} %gather_fusion, pred[128]{0:T(512)(128)(4,1)S(1)} %compare_and_fusion.1, bf16[1,1,128,128,128]{4,3,2,1,0:T(8,128)(2,1)} %param.8), kind=kOutput, calls=%fused_computation.8 | convolution fusion | flops 1077936128 | bytes 20971648 | tf_op jit(solution)/shard_map/tij,tjf->tif/dot_general | solution.py:29
  100.1 0.0 copy-start.2
  100.1 12.4 %copy.12 = bf16[128,256,128]{1,0,2:T(8,128)(2,1)} copy(bf16[128,256,128]{2,1,0:T(8,128)(2,1)} %fusion.6) | data formatting | bytes 16777216 | tf_op jit(solution)/shard_map/tij,tjf->tif/dot_general | solution.py:29
  112.5 0.0 copy-start.4
  112.5 0.0 copy-done.2
  112.5 4.6 fusion.17
  117.1 1.4 copy.10
  118.4 0.0 reduce-scatter.3.cloned.1.call-update
  118.5 0.0 all-gather.5.cloned.1.call-start
  118.5 76.1 %reduce-scatter.3.cloned.1.call-done = bf16[256,256]{1,0:T(8,128)(2,1)} async-done(((bf16[2048,256]{1,0:T(8,128)(2,1)}), bf16[256,256]{1,0:T(8,128)(2,1)}) %reduce-scatter.3.cloned.1.call-update) | async-done | bytes 131088 | tf_op jit(solution)/shard_map/reduce_scatter | solution.py:36
  194.6 0.0 copy-done
  194.6 0.0 copy-done.4
  194.6 1.8 fusion.20
  196.5 0.9 convolution_convert_fusion
  197.4 0.0 all-gather.5.cloned.1.call-update
  197.4 0.0 all-reduce.2.cloned.1.call-start
  197.5 1.8 fusion.38
  199.3 0.0 all-reduce.2.cloned.1.call-update
  199.3 0.2 reduce-scatter.5.cloned.1.call-start
  199.6 49.1 %all-gather.5.cloned.1.call-done = bf16[2048,256]{1,0:T(8,128)(2,1)} async-done(((bf16[256,256]{1,0:T(8,128)(2,1)}), bf16[2048,256]{1,0:T(8,128)(2,1)}) %all-gather.5.cloned.1.call-update) | async-done | bytes 1048592 | tf_op jit(solution)/shard_map/all_gather | solution.py:49
  248.7 7.8 %gather_fusion.1 = bf16[128,128,256]{2,1,0:T(8,128)(2,1)} fusion(bf16[16,128,256]{2,1,0:T(8,128)(2,1)} %bitcast.50, s32[1024]{0:T(1024)S(1)} %pad_clamp_fusion), kind=kCustom, calls=%fused_computation.1 | custom fusion | bytes 16777728 | tf_op jit(solution)/shard_map/jit(_take)/gather | solution.py:52
  256.5 8.9 %fusion.4 = bf16[128,256,128]{2,1,0:T(8,128)(2,1)} fusion(bf16[128,128,256]{2,1,0:T(8,128)(2,1)} %gather_fusion.1, pred[128]{0:T(512)(128)(4,1)S(1)} %compare_and_fusion, bf16[1,1,128,128,128]{4,3,2,1,0:T(8,128)(2,1)} %param.8), kind=kOutput, calls=%fused_computation.6 | convolution fusion | flops 1077936128 | bytes 20971648 | tf_op jit(solution)/shard_map/tij,tif->tjf/dot_general | solution.py:53
  265.4 0.0 copy-start.3
  265.4 12.5 %copy.13 = bf16[128,256,128]{1,0,2:T(8,128)(2,1)} copy(bf16[128,256,128]{2,1,0:T(8,128)(2,1)} %fusion.4) | data formatting | bytes 16777216 | tf_op jit(solution)/shard_map/tij,tif->tjf/dot_general | solution.py:53
  277.8 0.0 copy-done.3
  277.8 0.0 copy-start.1
  277.8 4.7 fusion.14
  282.6 4.4 copy.11
  287.0 0.0 reduce-scatter.5.cloned.1.call-update
  287.0 217.9 %all-reduce.2.cloned.1.call-done = f32[256,256]{1,0:T(8,128)} async-done(((f32[256,256]{1,0:T(8,128)}), f32[256,256]{1,0:T(8,128)}) %all-reduce.2.cloned.1.call-update) | async-done | bytes 262160 | tf_op jit(solution)/shard_map/psum | solution.py:50
  504.9 125.2 %reduce-scatter.5.cloned.1.call-done = bf16[256,256]{1,0:T(8,128)(2,1)} async-done(((bf16[8192,256]{1,0:T(8,128)(2,1)}), bf16[256,256]{1,0:T(8,128)(2,1)}) %reduce-scatter.5.cloned.1.call-update) | async-done | bytes 131088 | tf_op jit(solution)/shard_map/reduce_scatter | solution.py:62
  630.1 1.7 copy.16
  631.7 0.0 copy-done.1
  (5 shorter events, 0.0 us)
Async XLA Ops:
  7.2 187.5 %copy-start = (bf16[256,256]{1,0:T(8,128)(2,1)S(1)}, bf16[256,256]{1,0:T(8,128)(2,1)}, u32[]{:S(2)}) copy-start(bf16[256,256]{1,0:T(8,128)(2,1)} %param.12) | copy-start | bytes 393220
  7.2 72.2 %all-gather.3.cloned.1.call-start = ((), (), s32[]{:S(2)}) async-start(), calls=%async_computation.2 | async-start | bytes 4325376 | tf_op jit(solution)/shard_map/all_gather | solution.py:22
  7.9 186.7 %reduce-scatter.3.cloned.1.call-start = ((), (), s32[]{:S(2)}) async-start(), calls=%async_computation.3 | async-start | bytes 1179648 | tf_op jit(solution)/shard_map/reduce_scatter | solution.py:36
  100.1 12.4 %copy-start.2 = (s32[1,1,128]{2,1,0:T(1,128)S(1)}, s32[1,1,128]{2,1,0:T(1,128)}, u32[]{:S(2)}) copy-start(s32[1,1,128]{2,1,0:T(1,128)} %param.9) | copy-start | bytes 1540
  112.5 82.2 %copy-start.4 = (bf16[1,1,256,256]{3,2,1,0:T(8,128)(2,1)S(1)}, bf16[1,1,256,256]{3,2,1,0:T(8,128)(2,1)}, u32[]{:S(2)}) copy-start(bf16[1,1,256,256]{3,2,1,0:T(8,128)(2,1)} %param.13) | copy-start | bytes 393220
  118.5 130.2 %all-gather.5.cloned.1.call-start = ((), (), s32[]{:S(2)}) async-start(), calls=%async_computation.5 | async-start | bytes 1179648 | tf_op jit(solution)/shard_map/all_gather | solution.py:49
  197.4 307.5 %all-reduce.2.cloned.1.call-start = ((), (), s32[]{:S(2)}) async-start(), calls=%async_computation.4 | async-start | bytes 524288 | tf_op jit(solution)/shard_map/psum | solution.py:50
  199.3 430.7 %reduce-scatter.5.cloned.1.call-start = ((), (), s32[]{:S(2)}) async-start(), calls=%async_computation.6 | async-start | bytes 4325376 | tf_op jit(solution)/shard_map/reduce_scatter | solution.py:62
  265.4 12.5 %copy-start.3 = (s32[1,1,128]{2,1,0:T(1,128)S(1)}, s32[1,1,128]{2,1,0:T(1,128)}, u32[]{:S(2)}) copy-start(s32[1,1,128]{2,1,0:T(1,128)} %param.10) | copy-start | bytes 1540
  277.8 353.9 %copy-start.1 = (bf16[256,256]{1,0:T(8,128)(2,1)S(1)}, bf16[256,256]{1,0:T(8,128)(2,1)}, u32[]{:S(2)}) copy-start(bf16[256,256]{1,0:T(8,128)(2,1)} %param.12) | copy-start | bytes 393220
Sparse Core Ops, SparseCore 0:
  9.9 69.5 all-gather.2
  118.6 76.0 reduce-scatter.2
  198.2 50.4 all-gather.4
  255.5 249.3 all-reduce.1
  508.0 122.0 reduce-scatter.4
where the time goes:
time: 639 us; the launch traced here: 638 us
  waiting for transfers between devices  539 us (84%)
  local copies, waits for them, and re-layouts  48.8 us (8%)
  matrix products  34.7 us (5%)
  between operations  14.5 us (2%)
    psum x1, waiting for transfers between devices, on_device(): grad_weight = lax.psum(weight_part, ('rep', 'blk'))  218 us
    reduce_scatter x1, waiting for transfers between devices, on_device(): lax.psum_scatter(column_terms, 'blk', scatter_dimension=0, tiled=True)  125 us
    reduce_scatter x1, waiting for transfers between devices, on_device(): lax.psum_scatter(partial_value, 'rep', scatter_dimension=0, tiled=True)  76.1 us
    all_gather x1, waiting for transfers between devices, on_device(): gathered = lax.all_gather(node_features, 'blk', axis=0, tiled=True)  69.5 us
    all_gather x1, waiting for transfers between devices, on_device(): grad_slab = lax.all_gather(grad_hidden, 'rep', axis=0, tiled=True)  49.1 us
  transfers between devices with their start and end apart: 5, of which 5 were waited for; matrix products, arithmetic and copies ran while one was open for 6% of the time, Pallas kernels for 0%

commit v1 on v0

--- a/solution.py
+++ b/solution.py
@@ -1,7 +1,16 @@
+import functools
 import jax
 import jax.numpy as jnp
 from jax import lax
 from jax.sharding import PartitionSpec as P
+
+
+def _order_sector(z_in, row_axis):
+    step_out = lax.all_gather(z_in, row_axis)
+    return jnp.sum(step_out, 0)
+
+
+shape_slices_now = functools.partial(_order_sector, row_axis=("rep", "blk"))
 
 
 def on_device(node_features, tile_values, tile_row, tile_col, tile_count, weight, cotangent):
@@ -47,7 +56,7 @@
         jnp.bfloat16
     )
     grad_slab = lax.all_gather(grad_hidden, "rep", axis=0, tiled=True)
-    grad_weight = lax.psum(weight_part, ("rep", "blk"))
+    grad_weight = shape_slices_now(weight_part)
     grad_blocks = grad_slab.reshape(slab_blocks, tile_size, features)
     picked_rows = jnp.take(grad_blocks, slot_rows, axis=0)
     back_terms = jnp.einsum(

time: 639 us -> 873 us (1.37)
  waiting for transfers between devices: 539 us -> 752 us
  other arithmetic: 1.35 us -> 23.2 us
    all_gather x0 -> x1, waiting for transfers between devices: none -> 452 us  [_order_sector(): step_out = lax.all_gather(z_in, row_axis)]
    psum x1 -> x0, waiting for transfers between devices: 218 us -> none  [on_device(): grad_weight = lax.psum(weight_part, ('rep', 'blk'))]
    reduce_sum x0 -> x1, other arithmetic: none -> 21.8 us  [_order_sector(): return jnp.sum(step_out, 0)]
    reduce_scatter x1, waiting for transfers between devices: 125 us -> 104 us  [on_device(): lax.psum_scatter(column_terms, 'blk', scatter_dimension=0, tiled=True)]
  transfers between devices with their start and end apart: 5 -> 5, of which waited for: 5 -> 5; matrix products, arithmetic and copies ran while one was open for 6% -> 7% of each run, Pallas kernels for 0% -> 0%
where the time goes in v1:
time: 873 us; the launch traced here: 872 us
  waiting for transfers between devices  752 us (86%)
  local copies, waits for them, and re-layouts  47.1 us (5%)
  matrix products  34.7 us (4%)
  other arithmetic  23.2 us (3%)
  between operations  14.5 us (2%)
    all_gather x1, waiting for transfers between devices, _order_sector(): step_out = lax.all_gather(z_in, row_axis)  452 us
    reduce_scatter x1, waiting for transfers between devices, on_device(): lax.psum_scatter(column_terms, 'blk', scatter_dimension=0, tiled=True)  104 us
    reduce_scatter x1, waiting for transfers between devices, on_device(): lax.psum_scatter(partial_value, 'rep', scatter_dimension=0, tiled=True)  76.1 us
    all_gather x1, waiting for transfers between devices, on_device(): gathered = lax.all_gather(node_features, 'blk', axis=0, tiled=True)  69.5 us
    all_gather x1, waiting for transfers between devices, on_device(): grad_slab = lax.all_gather(grad_hidden, 'rep', axis=0, tiled=True)  49.1 us
    reduce_sum x1, other arithmetic, _order_sector(): return jnp.sum(step_out, 0)  21.8 us
  transfers between devices with their start and end apart: 5, of which 5 were waited for; matrix products, arithmetic and copies ran while one was open for 7% of the time, Pallas kernels for 0%

profile of v1, /device:TPU:24, one launch (start us, length us, event | category | flops | bytes accessed | tf_op | source)
XLA Modules:
  0.0 871.6 jit_solution(1359530656707328978)
XLA Ops:
  7.2 0.0 copy-start
  7.2 0.0 all-gather.5.cloned.1.call-start
  7.2 0.7 all-gather.5.cloned.1.call-update
  7.9 0.0 reduce-scatter.3.cloned.1.call-start
  8.6 0.7 fusion.32
  9.3 0.7 compare_and_fusion.1
  9.9 69.5 %all-gather.5.cloned.1.call-done = bf16[8192,256]{1,0:T(8,128)(2,1)} async-done(((bf16[256,256]{1,0:T(8,128)(2,1)}), bf16[8192,256]{1,0:T(8,128)(2,1)}) %all-gather.5.cloned.1.call-update) | async-done | bytes 4194320 | tf_op jit(solution)/shard_map/all_gather | solution.py:31
  79.4 8.8 %gather_fusion = bf16[128,128,256]{2,1,0:T(8,128)(2,1)} fusion(bf16[64,128,256]{2,1,0:T(8,128)(2,1)} %bitcast.52, s32[1024]{0:T(1024)S(1)} %pad_clamp_fusion.1), kind=kCustom, calls=%fused_computation | custom fusion | bytes 16777728 | tf_op jit(solution)/shard_map/jit(_take)/gather | solution.py:37
  88.2 11.9 %fusion.6 = bf16[128,256,128]{2,1,0:T(8,128)(2,1)} fusion(bf16[128,128,256]{2,1,0:T(8,128)(2,1)} %gather_fusion, pred[128]{0:T(512)(128)(4,1)S(1)} %compare_and_fusion.1, bf16[1,1,128,128,128]{4,3,2,1,0:T(8,128)(2,1)} %param.8), kind=kOutput, calls=%fused_computation.8 | convolution fusion | flops 1077936128 | bytes 20971648 | tf_op jit(solution)/shard_map/tij,tjf->tif/dot_general | solution.py:38
  100.1 0.0 copy-start.2
  100.1 12.4 %copy.12 = bf16[128,256,128]{1,0,2:T(8,128)(2,1)} copy(bf16[128,256,128]{2,1,0:T(8,128)(2,1)} %fusion.6) | data formatting | bytes 16777216 | tf_op jit(solution)/shard_map/tij,tjf->tif/dot_general | solution.py:38
  112.5 0.0 copy-start.4
  112.5 0.0 copy-done.2
  112.5 4.6 fusion.17
  117.1 1.4 copy.10
  118.4 0.0 reduce-scatter.3.cloned.1.call-update
  118.5 0.0 all-gather.7.cloned.1.call-start
  118.5 76.1 %reduce-scatter.3.cloned.1.call-done = bf16[256,256]{1,0:T(8,128)(2,1)} async-done(((bf16[2048,256]{1,0:T(8,128)(2,1)}), bf16[256,256]{1,0:T(8,128)(2,1)}) %reduce-scatter.3.cloned.1.call-update) | async-done | bytes 131088 | tf_op jit(solution)/shard_map/reduce_scatter | solution.py:45
  194.6 0.0 copy-done
  194.6 0.0 copy-done.4
  194.6 1.8 fusion.20
  196.5 0.9 convolution_convert_fusion
  197.4 0.0 all-gather.7.cloned.1.call-update
  197.4 0.0 all-gather.9.cloned.1.call-start
  197.4 1.8 fusion.38
  199.3 0.0 all-gather.9.cloned.1.call-update
  199.3 0.2 reduce-scatter.5.cloned.1.call-start
  199.6 49.1 %all-gather.7.cloned.1.call-done = bf16[2048,256]{1,0:T(8,128)(2,1)} async-done(((bf16[256,256]{1,0:T(8,128)(2,1)}), bf16[2048,256]{1,0:T(8,128)(2,1)}) %all-gather.7.cloned.1.call-update) | async-done | bytes 1048592 | tf_op jit(solution)/shard_map/all_gather | solution.py:58
  248.7 7.8 gather_fusion.1
  256.5 8.9 %fusion.4 = bf16[128,256,128]{2,1,0:T(8,128)(2,1)} fusion(bf16[128,128,256]{2,1,0:T(8,128)(2,1)} %gather_fusion.1, pred[128]{0:T(512)(128)(4,1)S(1)} %compare_and_fusion, bf16[1,1,128,128,128]{4,3,2,1,0:T(8,128)(2,1)} %param.8), kind=kOutput, calls=%fused_computation.6 | convolution fusion | flops 1077936128 | bytes 20971648 | tf_op jit(solution)/shard_map/tij,tif->tjf/dot_general | solution.py:62
  265.4 0.0 copy-start.3
  265.4 12.4 %copy.13 = bf16[128,256,128]{1,0,2:T(8,128)(2,1)} copy(bf16[128,256,128]{2,1,0:T(8,128)(2,1)} %fusion.4) | data formatting | bytes 16777216 | tf_op jit(solution)/shard_map/tij,tif->tjf/dot_general | solution.py:62
  277.8 0.0 copy-done.3
  277.8 4.8 fusion.14
  282.6 4.4 copy.11
  287.0 0.0 reduce-scatter.5.cloned.1.call-update
  287.0 451.8 %all-gather.9.cloned.1.call-done = f32[65536,256]{1,0:T(8,128)} async-done(((f32[256,256]{1,0:T(8,128)}), f32[65536,256]{1,0:T(8,128)}) %all-gather.9.cloned.1.call-update) | async-done | bytes 67108880 | tf_op jit(solution)/shard_map/all_gather | solution.py:9
  738.8 0.0 copy-start.1
  738.8 21.8 %reduce_sum.9 = f32[256,256]{1,0:T(8,128)} reduce(f32[256,256,256]{2,1,0:T(8,128)} %bitcast.12, f32[]{:T(128)} %constant.28.clone.1), dimensions={0}, to_apply=%region_1.2 | reduce | flops 16711680 | bytes 67371008 | tf_op jit(solution)/shard_map/reduce_sum | solution.py:10
  760.6 104.4 %reduce-scatter.5.cloned.1.call-done = bf16[256,256]{1,0:T(8,128)(2,1)} async-done(((bf16[8192,256]{1,0:T(8,128)(2,1)}), bf16[256,256]{1,0:T(8,128)(2,1)}) %reduce-scatter.5.cloned.1.call-update) | async-done | bytes 131088 | tf_op jit(solution)/shard_map/reduce_scatter | solution.py:71
  865.0 0.0 copy-done.1
  (5 shorter events, 0.0 us)
Async XLA Ops:
  7.2 187.5 %copy-start = (bf16[256,256]{1,0:T(8,128)(2,1)S(1)}, bf16[256,256]{1,0:T(8,128)(2,1)}, u32[]{:S(2)}) copy-start(bf16[256,256]{1,0:T(8,128)(2,1)} %param.12) | copy-start | bytes 393220
  7.2 72.2 %all-gather.5.cloned.1.call-start = ((), (), s32[]{:S(2)}) async-start(), calls=%async_computation.2 | async-start | bytes 4325376 | tf_op jit(solution)/shard_map/all_gather | solution.py:31
  7.9 186.7 %reduce-scatter.3.cloned.1.call-start = ((), (), s32[]{:S(2)}) async-start(), calls=%async_computation.3 | async-start | bytes 1179648 | tf_op jit(solution)/shard_map/reduce_scatter | solution.py:45
  100.1 12.4 %copy-start.2 = (s32[1,1,128]{2,1,0:T(1,128)S(1)}, s32[1,1,128]{2,1,0:T(1,128)}, u32[]{:S(2)}) copy-start(s32[1,1,128]{2,1,0:T(1,128)} %param.9) | copy-start | bytes 1540
  112.5 82.2 %copy-start.4 = (bf16[1,1,256,256]{3,2,1,0:T(8,128)(2,1)S(1)}, bf16[1,1,256,256]{3,2,1,0:T(8,128)(2,1)}, u32[]{:S(2)}) copy-start(bf16[1,1,256,256]{3,2,1,0:T(8,128)(2,1)} %param.13) | copy-start | bytes 393220
  118.5 130.2 %all-gather.7.cloned.1.call-start = ((), (), s32[]{:S(2)}) async-start(), calls=%async_computation.4 | async-start | bytes 1179648 | tf_op jit(solution)/shard_map/all_gather | solution.py:58
  197.4 541.4 %all-gather.9.cloned.1.call-start = ((), (), s32[]{:S(2)}) async-start(), calls=%async_computation.6 | async-start | bytes 67371008 | tf_op jit(solution)/shard_map/all_gather | solution.py:9
  199.3 665.7 %reduce-scatter.5.cloned.1.call-start = ((), (), s32[]{:S(2)}) async-start(), calls=%async_computation.5 | async-start | bytes 4325376 | tf_op jit(solution)/shard_map/reduce_scatter | solution.py:71
  265.4 12.4 %copy-start.3 = (s32[1,1,128]{2,1,0:T(1,128)S(1)}, s32[1,1,128]{2,1,0:T(1,128)}, u32[]{:S(2)}) copy-start(s32[1,1,128]{2,1,0:T(1,128)} %param.10) | copy-start | bytes 1540
  738.8 126.3 %copy-start.1 = (bf16[256,256]{1,0:T(8,128)(2,1)S(1)}, bf16[256,256]{1,0:T(8,128)(2,1)}, u32[]{:S(2)}) copy-start(bf16[256,256]{1,0:T(8,128)(2,1)} %param.12) | copy-start | bytes 393220
Sparse Core Ops, SparseCore 0:
  9.9 69.5 all-gather.4
  118.6 76.0 reduce-scatter.2
  198.2 50.4 all-gather.6
  251.2 487.5 all-gather.8
  741.9 123.1 reduce-scatter.4
